TPU v7x, 128 devices: a whole 4x4x4 slice. The times are simulated.
128 devices in a mesh: group: 4 (over y_lo, core), mp: 32 (over z, x, y_hi).
Axes of the slice: x: 4, y: 4 (y_hi: 2, y_lo: 2; y = y_hi * 2 + y_lo), z: 4, core: 2. Of those that a mesh axis runs over, the one named last changes fastest.
Arguments:
- tokens: bfloat16 [5120, 2048], P(('group', 'mp')), may hold values from -6 to 6
- lengths: int32 [4, 8], P('group'), may hold values from 1 to 512, 1280 in all within a row
- query_gain: float32 [2048], replicated, may hold values from 0.5 to 8
- key_gain: float32 [2048], replicated, may hold values from 0.5 to 8
- attn_post_gain: float32 [2048], replicated, may hold values from 0.5 to 1.5
- mlp_post_gain: float32 [2048], replicated, may hold values from 0.5 to 1.5
- query_weight: float32 [2048, 2048], P(('mp', 'group')), may hold values from -4 to 4
- key_weight: float32 [2048, 2048], P(('mp', 'group')), may hold values from -4 to 4
- value_weight: float32 [2048, 2048], P(('mp', 'group')), may hold values from -0.125 to 0.125
- output_weight: float32 [2048, 2048], P(('mp', 'group')), may hold values from -0.125 to 0.125
- gate_weight: float32 [2048, 8192], P(('mp', 'group')), may hold values from -0.125 to 0.125
- up_weight: float32 [2048, 8192], P(('mp', 'group')), may hold values from -0.125 to 0.125
- down_weight: float32 [8192, 2048], P(('mp', 'group')), may hold values from -0.0625 to 0.0625
Outputs:
- layer_out: bfloat16 [5120, 2048], P(('group', 'mp'))
Inputs may be any that keep to these rules, and one draw needn't show every extreme that they name: In each group the 8 prompt lengths sum to 1280; the longest is exactly 512.
All inputs are finite; a program needn't handle non-finite values.
Results may differ from a plain program's by a relative error of at most 0.034.
Values may be sent and summed in bfloat16 or wider, within the bound.
A program may use at most 64 MiB of HBM per device.

v0:
```python
import math
import jax
import jax.numpy as jnp
from jax import lax
from jax.sharding import Mesh, PartitionSpec as P

HEAD_DIM = 128
NORM_EPSILON = 1e-06
ROPE_BASE = 500000.0
PLANE = ("z", "x")
COLUMN = ("yhi", "ylo", "core")


def segments(prompt_lens, rows):
    seg_ends = jnp.cumsum(prompt_lens)
    starts = seg_ends - prompt_lens
    segment = jnp.sum((rows[:, None] >= seg_ends[None, :]).astype(jnp.int32), axis=1)
    member = segment[:, None] == jnp.arange(prompt_lens.shape[0], dtype=jnp.int32)[None, :]
    opening = jnp.sum(jnp.where(member, starts[None, :], 0), axis=1)
    return (segment, rows - opening)


def rotary(values_in, cosines, sines):
    half = HEAD_DIM // 2
    front, back = (values_in[:, :half], values_in[:, half:])
    return jnp.concatenate(
        [front * cosines - back * sines, back * cosines + front * sines], axis=-1
    )


def rms_scale(values_in, gain):
    return (
        values_in
        * lax.rsqrt(jnp.mean(values_in * values_in, axis=-1, keepdims=True) + NORM_EPSILON)
        * gain
    )


def sum_scatter(partial, tok_rows):
    blocks = partial.astype(jnp.bfloat16).reshape(-1, tok_rows, partial.shape[1])
    got = lax.all_to_all(blocks, PLANE, split_axis=0, concat_axis=0, tiled=True)
    return jnp.sum(got.astype(jnp.float32), axis=0)


def column_blocks(weights, parts):
    rows = weights[0].shape[0]
    split = [w.astype(jnp.bfloat16).reshape(rows, parts, -1) for w in weights]
    blocks = jnp.concatenate(split, axis=2).transpose(1, 0, 2)
    got = lax.all_to_all(blocks, PLANE, split_axis=0, concat_axis=0, tiled=True)
    whole = lax.all_gather(got, COLUMN, axis=1, tiled=True)
    return whole.reshape(-1, whole.shape[2])


def row_blocks(weight):
    return lax.all_gather(weight.astype(jnp.bfloat16), COLUMN, axis=0, tiled=True)


def per_device(
    tokens,
    lengths,
    query_gain,
    key_gain,
    attn_post_gain,
    mlp_post_gain,
    query_weight,
    key_weight,
    value_weight,
    output_weight,
    gate_weight,
    up_weight,
    down_weight,
):
    features = tokens.shape[1]
    parts = lax.axis_size("z") * lax.axis_size("x")
    place = lax.axis_index("z") * lax.axis_size("x") + lax.axis_index("x")
    half = lax.axis_index("yhi")
    tok_rows = tokens.shape[0]
    set_rows = tok_rows * parts
    qkv = column_blocks([query_weight, key_weight, value_weight], parts)
    output_block = row_blocks(output_weight)
    mlp_weights = column_blocks([gate_weight, up_weight], parts)
    down_block = row_blocks(down_weight)
    gathered = lax.all_gather(tokens, PLANE, axis=0, tiled=True)
    projected = jnp.dot(gathered, qkv, preferred_element_type=jnp.float32)
    q_raw, k_raw, v_raw = jnp.split(projected, 3, axis=1)
    squares = jnp.stack([jnp.sum(q_raw * q_raw, axis=1), jnp.sum(k_raw * k_raw, axis=1)])
    totals = jnp.sum(lax.all_gather(squares, PLANE, axis=0, tiled=False), axis=0)
    q_part = lax.dynamic_slice_in_dim(query_gain, place * HEAD_DIM, HEAD_DIM)
    k_part = lax.dynamic_slice_in_dim(key_gain, place * HEAD_DIM, HEAD_DIM)
    q_normed = q_raw * lax.rsqrt(totals[0] / features + NORM_EPSILON)[:, None] * q_part
    k_normed = k_raw * lax.rsqrt(totals[1] / features + NORM_EPSILON)[:, None] * k_part
    index = jnp.arange(set_rows, dtype=jnp.int32)

    def rows_of(which):
        return (index // tok_rows * 2 + which) * tok_rows + index % tok_rows

    my_rows = rows_of(half)
    segment, position = segments(lengths[0], my_rows)
    frequency = jnp.exp(
        jnp.arange(HEAD_DIM // 2, dtype=jnp.float32) * (-2.0 * math.log(ROPE_BASE) / HEAD_DIM)
    )
    angles = position.astype(jnp.float32)[:, None] * frequency[None, :]
    cosines, sines = (jnp.cos(angles), jnp.sin(angles))
    queries = rotary(q_normed, cosines, sines).astype(jnp.bfloat16)
    keys_rot = rotary(k_normed, cosines, sines).astype(jnp.bfloat16)
    kv_mine = jnp.concatenate([keys_rot, v_raw.astype(jnp.bfloat16)], axis=1)
    kv_other = lax.ppermute(kv_mine, "yhi", [(0, 1), (1, 0)])
    kv = jnp.concatenate([kv_mine, kv_other], axis=0)
    key_rows = jnp.concatenate([my_rows, rows_of(1 - half)])
    key_segment, _ = segments(lengths[0], key_rows)
    scores = lax.dot_general(
        queries, kv[:, :HEAD_DIM], (((1,), (1,)), ((), ())), preferred_element_type=jnp.float32
    ) * (1.0 / math.sqrt(HEAD_DIM))
    allowed = (segment[:, None] == key_segment[None, :]) & (key_rows[None, :] <= my_rows[:, None])
    scores = jnp.where(allowed, scores, -1e30)
    weights = jnp.exp(scores - jnp.max(scores, axis=1, keepdims=True))
    weights = weights / jnp.sum(weights, axis=1, keepdims=True)
    attended = jnp.dot(
        weights.astype(jnp.bfloat16), kv[:, HEAD_DIM:], preferred_element_type=jnp.float32
    ).astype(jnp.bfloat16)
    attn_out = sum_scatter(
        jnp.dot(attended, output_block, preferred_element_type=jnp.float32), tok_rows
    )
    hidden = (tokens.astype(jnp.float32) + rms_scale(attn_out, attn_post_gain)).astype(jnp.bfloat16)
    both_proj = jnp.dot(
        lax.all_gather(hidden, PLANE, axis=0, tiled=True),
        mlp_weights,
        preferred_element_type=jnp.float32,
    )
    width = both_proj.shape[1] // 2
    activated = (jax.nn.silu(both_proj[:, :width]) * both_proj[:, width:]).astype(jnp.bfloat16)
    mlp_out = sum_scatter(
        jnp.dot(activated, down_block, preferred_element_type=jnp.float32), tok_rows
    )
    return (hidden.astype(jnp.float32) + rms_scale(mlp_out, mlp_post_gain)).astype(jnp.bfloat16)


def solution(mesh):
    fine = Mesh(mesh.devices.reshape(2, 2, 4, 4, 2), ("ylo", "core", "z", "x", "yhi"))
    tok = P(("ylo", "core", "z", "x", "yhi"), None)
    weight = P(("z", "x", "yhi", "ylo", "core"), None)
    return jax.shard_map(
        per_device,
        mesh=fine,
        in_specs=(tok, P(("ylo", "core"), None), P(), P(), P(), P()) + (weight,) * 7,
        out_specs=tok,
        check_vma=False,
    )
```

profile of v0, /device:TPU:0, one launch (start us, length us, event | category | flops | bytes accessed | tf_op | source)
XLA Modules:
  0.0 315.3 jit_solution(8745225860466606189)
XLA Ops:
  6.5 1.0 convert_bitcast_fusion.2
  7.6 0.9 convert_bitcast_fusion.1
  8.5 0.9 convert_bitcast_fusion
  9.5 16.1 %all_to_all.20 = bf16[16,16,384]{2,1,0:T(8,128)(2,1)S(1)} all-to-all(bf16[16,16,384]{2,1,0:T(8,128)(2,1)S(1)} %copy.22), channel_id=1, replica_groups=mesh['ylo'=2,'core'=2,'z'=4,'x'=4,'yhi'=2] {'z','x'}, dimensions={0} | all-to-all | bytes 393216 | tf_op jit(solution)/shard_map/all_to_all | solution.py:49
  27.5 1.1 copy.25
  28.6 3.6 %all-to-all-start.2 = ((bf16[16,16,1024]{2,1,0:T(8,128)(2,1)}), bf16[16,16,1024]{2,1,0:T(8,128)(2,1)S(1)}, u32[]{:S(2)}, u32[]{:S(2)}) async-start(bf16[16,16,1024]{2,1,0:T(8,128)(2,1)} %copy.25), calls=%async_computation.2 | async-start | bytes 1048576 | tf_op jit(solution)/shard_map/all_to_all | solution.py:49
  32.3 10.3 %all-to-all-done.2 = bf16[16,16,1024]{2,1,0:T(8,128)(2,1)S(1)} async-done(((bf16[16,16,1024]{2,1,0:T(8,128)(2,1)}), bf16[16,16,1024]{2,1,0:T(8,128)(2,1)S(1)}, u32[]{:S(2)}, u32[]{:S(2)}) %all-to-all-start.2) | async-done | bytes 524320 | tf_op jit(solution)/shard_map/all_to_all | solution.py:49
  42.6 1.1 copy.26
  45.7 3.0 all-gather.8.cloned.1.call-done
  48.7 1.8 copy.24
  50.5 46.8 %all-gather.10.cloned.1.call-done = bf16[640,2048]{1,0:T(8,128)(2,1)} async-done(((bf16[40,2048]{1,0:T(8,128)(2,1)}), bf16[640,2048]{1,0:T(8,128)(2,1)}) %all-gather.10.cloned.1.call-update) | async-done | bytes 2621456 | tf_op jit(solution)/shard_map/all_gather | solution.py:83
  97.3 3.2 %convolution_bitcast_fusion = f32[640,384]{0,1:T(8,128)S(1)} fusion(bf16[2048,384]{1,0:T(8,128)(2,1)S(1)} %bitcast.42, bf16[640,2048]{1,0:T(8,128)(2,1)} %all-gather.10.cloned.1.call-done), kind=kOutput, calls=%fused_computation.10 | convolution fusion | flops 1006632960 | bytes 5177344 | tf_op jit(solution)/shard_map/dot_general | solution.py:84
  100.6 22.9 %all-gather.1 = f32[16,2,640]{2,1,0:T(2,128)S(1)} all-gather(f32[1,2,640]{2,1,0:T(2,128)S(1)} %maximum_bitcast_fusion.2), channel_id=2, replica_groups=mesh['ylo'=2,'core'=2,'z'=4,'x'=4,'yhi'=2] {'z','x'}, dimensions={0}, use_global_device_ids=true | all-gather | bytes 87040 | tf_op jit(solution)/shard_map/all_gather | solution.py:87
  124.5 3.1 collective-permute-start
  127.7 17.3 %all_gather.28 = bf16[128,2048]{1,0:T(8,128)(2,1)} all-gather(bf16[16,2048]{1,0:T(8,128)(2,1)S(1)} %convert_element_type.79), channel_id=1, replica_groups=mesh['ylo'=2,'core'=2,'z'=4,'x'=4,'yhi'=2] {'yhi','ylo','core'}, dimensions={0}, use_global_device_ids=true | all-gather | bytes 589824 | tf_op jit(solution)/shard_map/all_gather | solution.py:55
  145.1 1.0 fusion.48
  146.7 4.9 %convolution_convert_fusion.1 = bf16[640,2048]{1,0:T(8,128)(2,1)} fusion(bf16[128,2048]{1,0:T(8,128)(2,1)} %all_gather.28, f32[640,1280]{1,0:T(8,128)S(1)} %get-tuple-element.18, f32[640]{0:T(1024)S(1)} %fusion.1, f32[640]{0:T(1024)S(1)} %get-tuple-element.17, bf16[1280,256]{0,1:T(8,128)(2,1)} %copy-done.1), kind=kOutput, calls=%fused_computation.7 | convolution fusion | flops 549109760 | bytes 6755328 | tf_op jit(solution)/shard_map/dot_general | solution.py:122
  151.6 40.8 %all_to_all.21 = bf16[16,40,2048]{2,1,0:T(8,128)(2,1)S(1)} all-to-all(bf16[16,40,2048]{2,1,0:T(8,128)(2,1)} %bitcast.40), channel_id=1, replica_groups=mesh['ylo'=2,'core'=2,'z'=4,'x'=4,'yhi'=2] {'z','x'}, dimensions={0} | all-to-all | bytes 5242880 | tf_op jit(solution)/shard_map/all_to_all | solution.py:41
  195.1 6.5 %copy.27 = bf16[16,128,1024]{2,1,0:T(8,128)(2,1)} copy(bf16[16,128,1024]{2,0,1:T(8,128)(2,1)} %all-gather.14.cloned.1.call-done) | data formatting | bytes 8388608 | tf_op jit(solution)/shard_map/all_gather | solution.py:50
  201.6 35.2 %all-gather.12.cloned.1.call-done = bf16[640,2048]{1,0:T(8,128)(2,1)} async-done(((bf16[40,2048]{1,0:T(8,128)(2,1)}), bf16[640,2048]{1,0:T(8,128)(2,1)}) %all-gather.12.cloned.1.call-update) | async-done | bytes 2621456 | tf_op jit(solution)/shard_map/all_gather | solution.py:126
  236.8 5.4 %fusion.49 = f32[640,1024]{1,0:T(8,128)S(1)} fusion(bf16[640,2048]{1,0:T(8,128)(2,1)} %all-gather.12.cloned.1.call-done, bf16[2048,1024]{1,0:T(8,128)(2,1)} %bitcast.39), kind=kOutput, calls=%fused_computation.91 | convolution fusion | flops 2684354560 | bytes 9437184 | tf_op jit(solution)/shard_map/dot_general | solution.py:125
  242.2 20.6 %all-gather.16.cloned.1.call-done = bf16[512,2048]{1,0:T(8,128)(2,1)} async-done(((bf16[64,2048]{1,0:T(8,128)(2,1)}), bf16[512,2048]{1,0:T(8,128)(2,1)}) %all-gather.16.cloned.1.call-update) | async-done | bytes 2097168 | tf_op jit(solution)/shard_map/all_gather | solution.py:55
  262.8 3.1 convolution_convert_fusion
  265.9 41.2 %all_to_all.22 = bf16[16,40,2048]{2,1,0:T(8,128)(2,1)S(1)} all-to-all(bf16[16,40,2048]{2,1,0:T(8,128)(2,1)S(1)} %bitcast.41), channel_id=1, replica_groups=mesh['ylo'=2,'core'=2,'z'=4,'x'=4,'yhi'=2] {'z','x'}, dimensions={0} | all-to-all | bytes 5242880 | tf_op jit(solution)/shard_map/all_to_all | solution.py:41
  (77 shorter events, 10.1 us)
Async XLA Ops:
  6.5 20.6 %copy-start.3 = (f32[16,8192]{1,0:T(8,128)S(1)}, f32[16,8192]{1,0:T(8,128)}, u32[]{:S(2)}) copy-start(f32[16,8192]{1,0:T(8,128)} %param.23) | copy-start | bytes 1572868
  6.5 20.7 %copy-start.4 = (f32[16,8192]{1,0:T(8,128)S(1)}, f32[16,8192]{1,0:T(8,128)}, u32[]{:S(2)}) copy-start(f32[16,8192]{1,0:T(8,128)} %param.24) | copy-start | bytes 1572868
  6.5 42.2 %all-gather.8.cloned.1.call-start = ((), (), s32[]{:S(2)}) async-start(), calls=%async_computation.4 | async-start | bytes 1769472 | tf_op jit(solution)/shard_map/all_gather | solution.py:50
  26.4 70.9 %all-gather.10.cloned.1.call-start = ((), (), s32[]{:S(2)}) async-start(), calls=%async_computation.5 | async-start | bytes 2785280 | tf_op jit(solution)/shard_map/all_gather | solution.py:83
  27.3 18.0 %copy-start.9 = (s32[1,8]{1,0:T(1,128)S(1)}, s32[1,8]{1,0:T(1,128)}, u32[]{:S(2)}) copy-start(s32[1,8]{1,0:T(1,128)} %param.14) | copy-start | bytes 100
  27.3 18.2 %copy-start.6 = (f32[16,2048]{1,0:T(8,128)S(1)}, f32[16,2048]{1,0:T(8,128)}, u32[]{:S(2)}) copy-start(f32[16,2048]{1,0:T(8,128)} %param.22) | copy-start | bytes 393220
  28.6 14.0 %all-to-all-start.2 = ((bf16[16,16,1024]{2,1,0:T(8,128)(2,1)}), bf16[16,16,1024]{2,1,0:T(8,128)(2,1)S(1)}, u32[]{:S(2)}, u32[]{:S(2)}) async-start(bf16[16,16,1024]{2,1,0:T(8,128)(2,1)} %copy.25), calls=%async_computation.2 | async-start | bytes 1048576 | tf_op jit(solution)/shard_map/all_to_all | solution.py:49
  32.2 163.0 %all-gather.14.cloned.1.call-start = ((), (), s32[]{:S(2)}) async-start(), calls=%async_computation.7 | async-start | bytes 4718592 | tf_op jit(solution)/shard_map/all_gather | solution.py:50
  43.7 193.1 %all-gather.12.cloned.1.call-start = ((), (), s32[]{:S(2)}) async-start(), calls=%async_computation.6 | async-start | bytes 2785280 | tf_op jit(solution)/shard_map/all_gather | solution.py:126
  124.5 20.5 %collective-permute-start = (bf16[640,256]{0,1:T(8,128)(2,1)S(1)}, bf16[640,256]{0,1:T(8,128)(2,1)S(1)}, u32[]{:S(2)}, u32[]{:S(2)}) collective-permute-start(bf16[640,256]{0,1:T(8,128)(2,1)S(1)} %pad_maximum_fusion.1), channel_id=1, source_target_pairs={{0,1},{1,0},{2,3},{3,2},{4,5},{5,4},{6,7},{7,6},{8,9},{9,8},{10,11... | collective-permute-start | bytes 983048 | tf_op jit(solution)/shard_map/ppermute | solution.py:107
  145.1 1.1 copy-start.1
  192.4 0.9 copy-start.2
  192.4 0.9 copy-start.7
  192.4 2.0 copy-start.5
  194.1 68.7 %all-gather.16.cloned.1.call-start = ((), (), s32[]{:S(2)}) async-start(), calls=%async_computation.8 | async-start | bytes 2359296 | tf_op jit(solution)/shard_map/all_gather | solution.py:55
  307.1 0.9 copy-start
  307.1 0.9 copy-start.8
Sparse Core Ops, SparseCore 0:
  26.5 22.1 all-gather.7
  50.9 46.3 all-gather.9
  99.0 36.7 all-gather.13
  194.2 42.4 all-gather.11
  238.3 24.4 all-gather.15
where the time goes:
time: 316 us; the launch traced here: 315 us
  blocking collectives  138 us (44%)
  waiting for transfers between devices  117 us (37%)
  matrix products  17.6 us (6%)
  local copies, waits for them, and re-layouts  13.6 us (4%)
  between operations  13.5 us (4%)
  other arithmetic  8.72 us (3%)
  starting transfers between devices  7.01 us (2%)
    all_to_all x2, blocking collectives, sum_scatter(): got = lax.all_to_all(blocks, PLANE, split_axis=0, concat_axis=0, tiled=True)  82 us
    all_gather x1, waiting for transfers between devices, per_device(): gathered = lax.all_gather(tokens, PLANE, axis=0, tiled=True)  46.8 us
    all_gather x1, waiting for transfers between devices, per_device(): lax.all_gather(hidden, PLANE, axis=0, tiled=True)  35.2 us
    all_gather x1, blocking collectives, per_device(): lax.all_gather(squares, PLANE, axis=0, tiled=False)  22.9 us
    all_gather x1, waiting for transfers between devices, row_blocks(): lax.all_gather(weight.astype(jnp.bfloat16), COLUMN, axis=0, tiled=True)  20.6 us
    all_gather x1, blocking collectives, row_blocks(): lax.all_gather(weight.astype(jnp.bfloat16), COLUMN, axis=0, tiled=True)  17.3 us
    all_to_all x1, blocking collectives, column_blocks(): got = lax.all_to_all(blocks, PLANE, split_axis=0, concat_axis=0, tiled=True)  16.1 us
    all_to_all x1, waiting for transfers between devices, column_blocks(): got = lax.all_to_all(blocks, PLANE, split_axis=0, concat_axis=0, tiled=True)  10.3 us
  transfers between devices with their start and end apart: 7, of which 5 were waited for; matrix products, arithmetic and copies ran while one was open for 10% of the time, Pallas kernels for 0%

commit v1 on v0

--- a/solution.py
+++ b/solution.py
@@ -47,7 +47,9 @@
     split = [w.astype(jnp.bfloat16).reshape(rows, parts, -1) for w in weights]
     blocks = jnp.concatenate(split, axis=2).transpose(1, 0, 2)
     got = lax.all_to_all(blocks, PLANE, split_axis=0, concat_axis=0, tiled=True)
-    whole = lax.all_gather(got, COLUMN, axis=1, tiled=True)
+    whole = jnp.concatenate(
+        lax.all_to_all(jnp.stack([got] * lax.axis_size(COLUMN)), COLUMN, 0, 0), axis=1
+    )
     return whole.reshape(-1, whole.shape[2])
 
 

time: 316 us -> 291 us (0.921)
  waiting for transfers between devices: 117 us -> 82.7 us
  blocking collectives: 138 us -> 145 us
  starting transfers between devices: 7.01 us -> 12.5 us
    all_to_all x1 -> x2, waiting for transfers between devices: 10.3 us -> 76.6 us  [column_blocks(): lax.all_to_all(jnp.stack([got] * lax.axis_size(COLUMN)), COLUMN, 0, 0)]
    all_gather x1, waiting for transfers between devices: 46.8 us -> 5.35 us  [per_device(): gathered = lax.all_gather(tokens, PLANE, axis=0, tiled=True)]
    all_gather x1, waiting for transfers between devices: 35.2 us -> 0.01 us  [per_device(): lax.all_gather(hidden, PLANE, axis=0, tiled=True)]
    all_gather x1, waiting for transfers between devices: 20.6 us -> 0.02 us  [row_blocks(): lax.all_gather(weight.astype(jnp.bfloat16), COLUMN, axis=0, tiled=True)]
    all_to_all x1 -> x2, blocking collectives: 16.1 us -> 31.1 us  [column_blocks(): got = lax.all_to_all(blocks, PLANE, split_axis=0, concat_axis=0, tiled=True)]
    all_gather x2 -> x0, local copies, waits for them, and re-layouts: 8.25 us -> none  [column_blocks(): whole = lax.all_gather(got, COLUMN, axis=1, tiled=True)]
    all_to_all x2, blocking collectives: 82 us -> 75.3 us  [sum_scatter(): got = lax.all_to_all(blocks, PLANE, split_axis=0, concat_axis=0, tiled=True)]
    all_to_all x1 -> x2, starting transfers between devices: 3.57 us -> 9.15 us  [column_blocks(): lax.all_to_all(jnp.stack([got] * lax.axis_size(COLUMN)), COLUMN, 0, 0)]
  transfers between devices with their start and end apart: 7 -> 6, of which waited for: 5 -> 3; matrix products, arithmetic and copies ran while one was open for 10% -> 7% of each run, Pallas kernels for 0% -> 0%
where the time goes in v1:
time: 291 us; the launch traced here: 290 us
  blocking collectives  145 us (50%)
  waiting for transfers between devices  82.7 us (28%)
  matrix products  17.6 us (6%)
  between operations  13.4 us (5%)
  starting transfers between devices  12.5 us (4%)
  local copies, waits for them, and re-layouts  11.2 us (4%)
  other arithmetic  7.82 us (3%)
    all_to_all x2, waiting for transfers between devices, column_blocks(): lax.all_to_all(jnp.stack([got] * lax.axis_size(COLUMN)), COLUMN, 0, 0)  76.6 us
    all_to_all x2, blocking collectives, sum_scatter(): got = lax.all_to_all(blocks, PLANE, split_axis=0, concat_axis=0, tiled=True)  75.3 us
    all_to_all x2, blocking collectives, column_blocks(): got = lax.all_to_all(blocks, PLANE, split_axis=0, concat_axis=0, tiled=True)  31.1 us
    all_gather x1, blocking collectives, per_device(): lax.all_gather(squares, PLANE, axis=0, tiled=False)  23 us
    all_gather x1, blocking collectives, row_blocks(): lax.all_gather(weight.astype(jnp.bfloat16), COLUMN, axis=0, tiled=True)  15.2 us
    all_to_all x2, starting transfers between devices, column_blocks(): lax.all_to_all(jnp.stack([got] * lax.axis_size(COLUMN)), COLUMN, 0, 0)  9.15 us
  transfers between devices with their start and end apart: 6, of which 3 were waited for; matrix products, arithmetic and copies ran while one was open for 7% of the time, Pallas kernels for 0%

profile of v1, /device:TPU:0, one launch (start us, length us, event | category | flops | bytes accessed | tf_op | source)
XLA Modules:
  0.0 289.8 jit_solution(13893176333669941131)
XLA Ops:
  7.3 0.9 copy_bitcast_fusion.4
  8.2 1.0 copy_bitcast_fusion.2
  9.2 16.2 %all_to_all.30 = bf16[16,16,384]{2,1,0:T(8,128)(2,1)S(1)} all-to-all(bf16[16,16,384]{2,1,0:T(8,128)(2,1)S(1)} %maximum_bitcast_fusion.1), channel_id=1, replica_groups=mesh['ylo'=2,'core'=2,'z'=4,'x'=4,'yhi'=2] {'z','x'}, dimensions={0} | all-to-all | bytes 393216 | tf_op jit(solution)/shard_map/all_to_all | solution.py:49
  25.5 1.3 stack.10
  26.7 4.5 %all-to-all-start.1 = ((bf16[8,16,16,384]{3,2,1,0:T(8,128)(2,1)}), bf16[8,16,16,384]{3,2,1,0:T(8,128)(2,1)S(1)}, u32[]{:S(2)}, u32[]{:S(2)}) async-start(bf16[8,16,16,384]{3,2,1,0:T(8,128)(2,1)} %stack.10), calls=%async_computation.1 | async-start | bytes 3145728 | tf_op jit(solution)/shard_map/all_to_all | solution.py:51
  33.3 19.5 %all-to-all-done.1 = bf16[8,16,16,384]{3,2,1,0:T(8,128)(2,1)S(1)} async-done(((bf16[8,16,16,384]{3,2,1,0:T(8,128)(2,1)}), bf16[8,16,16,384]{3,2,1,0:T(8,128)(2,1)S(1)}, u32[]{:S(2)}, u32[]{:S(2)}) %all-to-all-start.1) | async-done | bytes 1572896 | tf_op jit(solution)/shard_map/all_to_all | solution.py:51
  53.0 5.3 %all-gather.6.cloned.1.call-done = bf16[640,2048]{1,0:T(8,128)(2,1)} async-done(((bf16[40,2048]{1,0:T(8,128)(2,1)}), bf16[640,2048]{1,0:T(8,128)(2,1)}) %all-gather.6.cloned.1.call-update) | async-done | bytes 2621456 | tf_op jit(solution)/shard_map/all_gather | solution.py:85
  58.4 3.2 %convolution_bitcast_fusion = f32[640,384]{0,1:T(8,128)S(1)} fusion(bf16[2048,384]{1,0:T(8,128)(2,1)S(1)} %bitcast.54, bf16[640,2048]{1,0:T(8,128)(2,1)} %all-gather.6.cloned.1.call-done), kind=kOutput, calls=%fused_computation.10 | convolution fusion | flops 1006632960 | bytes 5177344 | tf_op jit(solution)/shard_map/dot_general | solution.py:86
  61.7 23.0 %all-gather.1 = f32[16,2,640]{2,1,0:T(2,128)S(1)} all-gather(f32[1,2,640]{2,1,0:T(2,128)S(1)} %maximum_bitcast_fusion.2), channel_id=2, replica_groups=mesh['ylo'=2,'core'=2,'z'=4,'x'=4,'yhi'=2] {'z','x'}, dimensions={0}, use_global_device_ids=true | all-gather | bytes 87040 | tf_op jit(solution)/shard_map/all_gather | solution.py:89
  85.6 3.1 %collective-permute-start = (bf16[640,256]{0,1:T(8,128)(2,1)S(1)}, bf16[640,256]{0,1:T(8,128)(2,1)S(1)}, u32[]{:S(2)}, u32[]{:S(2)}) collective-permute-start(bf16[640,256]{0,1:T(8,128)(2,1)S(1)} %pad_maximum_fusion.1), channel_id=1, source_target_pairs={{0,1},{1,0},{2,3},{3,2},{4,5},{5,4},{6,7},{7,6},{8,9},{9,8},{10,11... | collective-permute-start | bytes 983048 | tf_op jit(solution)/shard_map/ppermute | solution.py:109
  88.8 15.2 %all_gather.21 = bf16[128,2048]{1,0:T(8,128)(2,1)} all-gather(bf16[16,2048]{1,0:T(8,128)(2,1)S(1)} %convert_element_type.79), channel_id=1, replica_groups=mesh['ylo'=2,'core'=2,'z'=4,'x'=4,'yhi'=2] {'yhi','ylo','core'}, dimensions={0}, use_global_device_ids=true | all-gather | bytes 589824 | tf_op jit(solution)/shard_map/all_gather | solution.py:57
  104.1 1.1 fusion.48
  105.7 4.8 %convolution_convert_fusion.1 = bf16[640,2048]{1,0:T(8,128)(2,1)} fusion(bf16[128,2048]{1,0:T(8,128)(2,1)} %all_gather.21, f32[640,1280]{1,0:T(8,128)S(1)} %get-tuple-element.18, f32[640]{0:T(1024)S(1)} %fusion.1, f32[640]{0:T(1024)S(1)} %get-tuple-element.17, bf16[1280,256]{0,1:T(8,128)(2,1)} %copy-done.1), kind=kOutput, calls=%fused_computation.7 | convolution fusion | flops 549109760 | bytes 6755328 | tf_op jit(solution)/shard_map/dot_general | solution.py:124
  110.6 38.6 %all_to_all.31 = bf16[16,40,2048]{2,1,0:T(8,128)(2,1)S(1)} all-to-all(bf16[16,40,2048]{2,1,0:T(8,128)(2,1)} %bitcast.52), channel_id=1, replica_groups=mesh['ylo'=2,'core'=2,'z'=4,'x'=4,'yhi'=2] {'z','x'}, dimensions={0} | all-to-all | bytes 5242880 | tf_op jit(solution)/shard_map/all_to_all | solution.py:41
  150.1 0.8 add_convert_fusion.1
  151.1 14.9 %all_to_all.32 = bf16[16,16,1024]{2,1,0:T(8,128)(2,1)S(1)} all-to-all(bf16[16,16,1024]{2,1,0:T(8,128)(2,1)S(1)} %maximum_bitcast_fusion), channel_id=1, replica_groups=mesh['ylo'=2,'core'=2,'z'=4,'x'=4,'yhi'=2] {'z','x'}, dimensions={0} | all-to-all | bytes 1048576 | tf_op jit(solution)/shard_map/all_to_all | solution.py:49
  165.9 2.5 stack.14
  168.5 4.7 %all-to-all-start.4 = ((bf16[8,16,16,1024]{3,2,1,0:T(8,128)(2,1)}), bf16[8,16,16,1024]{3,2,1,0:T(8,128)(2,1)}, u32[]{:S(2)}, u32[]{:S(2)}) async-start(bf16[8,16,16,1024]{3,2,1,0:T(8,128)(2,1)} %stack.14), calls=%async_computation.4 | async-start | bytes 8388608 | tf_op jit(solution)/shard_map/all_to_all | solution.py:51
  174.2 57.1 %all-to-all-done.4 = bf16[8,16,16,1024]{3,2,1,0:T(8,128)(2,1)} async-done(((bf16[8,16,16,1024]{3,2,1,0:T(8,128)(2,1)}), bf16[8,16,16,1024]{3,2,1,0:T(8,128)(2,1)}, u32[]{:S(2)}, u32[]{:S(2)}) %all-to-all-start.4) | async-done | bytes 4194336 | tf_op jit(solution)/shard_map/all_to_all | solution.py:51
  231.2 5.0 %copy.34 = bf16[8,16,16,1024]{3,2,0,1:T(8,128)(2,1)} copy(bf16[8,16,16,1024]{3,2,1,0:T(8,128)(2,1)} %all-to-all-done.4) | data formatting | bytes 8388608 | tf_op jit(solution)/shard_map/all_to_all | solution.py:51
  236.2 5.4 %fusion.49 = f32[640,1024]{1,0:T(8,128)S(1)} fusion(bf16[640,2048]{1,0:T(8,128)(2,1)} %all-gather.8.cloned.1.call-done, bf16[2048,1024]{1,0:T(8,128)(2,1)} %bitcast.51), kind=kOutput, calls=%fused_computation.96 | convolution fusion | flops 2684354560 | bytes 9437184 | tf_op jit(solution)/shard_map/dot_general | solution.py:127
  241.7 3.1 %convolution_convert_fusion = bf16[640,2048]{1,0:T(8,128)(2,1)S(1)} fusion(bf16[512,2048]{1,0:T(8,128)(2,1)} %all-gather.10.cloned.1.call-done, f32[640,1024]{1,0:T(8,128)S(1)} %fusion.49), kind=kOutput, calls=%fused_computation.6 | convolution fusion | flops 1345454080 | bytes 7340032 | tf_op jit(solution)/shard_map/dot_general | solution.py:135
  244.9 36.7 %all_to_all.33 = bf16[16,40,2048]{2,1,0:T(8,128)(2,1)S(1)} all-to-all(bf16[16,40,2048]{2,1,0:T(8,128)(2,1)S(1)} %bitcast.53), channel_id=1, replica_groups=mesh['ylo'=2,'core'=2,'z'=4,'x'=4,'yhi'=2] {'z','x'}, dimensions={0} | all-to-all | bytes 5242880 | tf_op jit(solution)/shard_map/all_to_all | solution.py:41
  282.5 0.8 add_convert_fusion
  (67 shorter events, 7.8 us)
Async XLA Ops:
  6.5 51.8 %all-gather.6.cloned.1.call-start = ((), (), s32[]{:S(2)}) async-start(), calls=%async_computation.6 | async-start | bytes 2785280 | tf_op jit(solution)/shard_map/all_gather | solution.py:85
  9.2 23.6 %copy-start.9 = (s32[1,8]{1,0:T(1,128)S(1)}, s32[1,8]{1,0:T(1,128)}, u32[]{:S(2)}) copy-start(s32[1,8]{1,0:T(1,128)} %param.14) | copy-start | bytes 100
  9.2 23.8 %copy-start.6 = (f32[16,2048]{1,0:T(8,128)S(1)}, f32[16,2048]{1,0:T(8,128)}, u32[]{:S(2)}) copy-start(f32[16,2048]{1,0:T(8,128)} %param.22) | copy-start | bytes 393220
  26.7 26.1 %all-to-all-start.1 = ((bf16[8,16,16,384]{3,2,1,0:T(8,128)(2,1)}), bf16[8,16,16,384]{3,2,1,0:T(8,128)(2,1)S(1)}, u32[]{:S(2)}, u32[]{:S(2)}) async-start(bf16[8,16,16,384]{3,2,1,0:T(8,128)(2,1)} %stack.10), calls=%async_computation.1 | async-start | bytes 3145728 | tf_op jit(solution)/shard_map/all_to_all | solution.py:51
  31.2 205.0 %all-gather.8.cloned.1.call-start = ((), (), s32[]{:S(2)}) async-start(), calls=%async_computation.7 | async-start | bytes 2785280 | tf_op jit(solution)/shard_map/all_gather | solution.py:128
  85.6 18.4 %collective-permute-start = (bf16[640,256]{0,1:T(8,128)(2,1)S(1)}, bf16[640,256]{0,1:T(8,128)(2,1)S(1)}, u32[]{:S(2)}, u32[]{:S(2)}) collective-permute-start(bf16[640,256]{0,1:T(8,128)(2,1)S(1)} %pad_maximum_fusion.1), channel_id=1, source_target_pairs={{0,1},{1,0},{2,3},{3,2},{4,5},{5,4},{6,7},{7,6},{8,9},{9,8},{10,11... | collective-permute-start | bytes 983048 | tf_op jit(solution)/shard_map/ppermute | solution.py:109
  104.1 1.1 copy-start.1
  149.1 0.9 copy-start.2
  149.2 0.9 copy-start.7
  149.2 1.7 copy-start.3
  149.2 1.8 copy-start.4
  168.5 4.9 %copy-start.5 = (f32[64,2048]{1,0:T(8,128)S(1)}, f32[64,2048]{1,0:T(8,128)}, u32[]{:S(2)}) copy-start(f32[64,2048]{1,0:T(8,128)} %param.25) | copy-start | bytes 1572868
  168.5 62.8 %all-to-all-start.4 = ((bf16[8,16,16,1024]{3,2,1,0:T(8,128)(2,1)}), bf16[8,16,16,1024]{3,2,1,0:T(8,128)(2,1)}, u32[]{:S(2)}, u32[]{:S(2)}) async-start(bf16[8,16,16,1024]{3,2,1,0:T(8,128)(2,1)} %stack.14), calls=%async_computation.4 | async-start | bytes 8388608 | tf_op jit(solution)/shard_map/all_to_all | solution.py:51
  173.1 68.6 %all-gather.10.cloned.1.call-start = ((), (), s32[]{:S(2)}) async-start(), calls=%async_computation.8 | async-start | bytes 2359296 | tf_op jit(solution)/shard_map/all_gather | solution.py:57
  281.6 0.9 copy-start
  281.6 0.9 copy-start.8
Sparse Core Ops, SparseCore 0:
  9.5 48.8 all-gather.5
  151.0 43.2 all-gather.7
  196.0 30.9 all-gather.9
